TPU v7x, 256 devices: a whole 4x4x8 slice. The times are simulated.
256 devices in a mesh: seq: 16 (over y, x), fsdp: 16 (over z, core).
Axes of the slice: x: 4, y: 4, z: 8, core: 2. Of those that a mesh axis runs over, the one named last changes fastest.
Arguments:
- kv_cache: bfloat16 [2, 32, 8192, 1280], P(None, 'fsdp', 'seq'), may hold values from -6 to 6
- keep_flags: int32 [32, 8192], P('fsdp', 'seq'), may hold values from 0 to 1, as said below
- block_weights: float32 [32, 8192], P('fsdp', 'seq'), may hold values from 0.05 to 2
- lengths: int32 [32], P('fsdp'), may hold values from 2048 to 8192, as said below
- token_qkv: bfloat16 [32, 3840], P('fsdp'), may hold values from -10 to 10
- stream: bfloat16 [32, 1280], P('fsdp'), may hold values from -0.59765625 to 0.59765625
- w_out: bfloat16 [1280, 1280], P(None, 'fsdp'), may hold values from -0.15625 to 0.15625
- w_up: bfloat16 [1280, 1280], P(None, 'fsdp'), may hold values from -0.15625 to 0.15625
- w_down: bfloat16 [1280, 1280], P(None, 'fsdp'), may hold values from -0.15625 to 0.15625
- w_qkv: bfloat16 [1280, 3840], P(None, 'fsdp'), may hold values from -0.15625 to 0.15625
- mlp_gain: float32 [1280], replicated, may hold values from 0.1 to 1.9
- next_gain: float32 [1280], replicated, may hold values from 0.1 to 1.9
Outputs:
- packed_cache: bfloat16 [2, 32, 8192, 1280], P(None, 'fsdp', 'seq')
- block_summary: bfloat16 [2, 32, 512, 1280], P(None, 'fsdp', 'seq')
- layer_out: bfloat16 [32, 1280], P('fsdp', 'seq')
- next_qkv: bfloat16 [32, 3840], P('fsdp', 'seq')
Inputs may be any that keep to these rules, and one draw needn't show every extreme that they name: `keep_flags`: in every draw one request keeps all 512 positions of one aligned block of 512 positions. `lengths`: in every draw some request has 8192 filled positions.
All inputs are finite; a program needn't handle non-finite values.
Results may differ from a plain program's by a relative error of at most 0.02.
Values may be sent and summed in bfloat16 or wider, within the bound.
A program may use at most 128 MiB of HBM per device.

v0:
```python
import math
import jax
import jax.numpy as jnp
from jax import lax
from jax.sharding import PartitionSpec as P

H = 16
BLK = 16
neg_fill = -1e30


def combined_all(part, axis, combine):
    gathered = jax.tree.map(lambda a: lax.all_gather(a, axis), part)

    def take(source):
        return jax.tree.map(lambda a: lax.dynamic_index_in_dim(a, source, 0, False), gathered)

    return lax.fori_loop(
        1, lax.axis_size(axis), lambda source, state: combine(state, take(source)), take(0)
    )


def normalize(values, gain):
    wide = values.astype(jnp.float32)
    factor = lax.rsqrt(jnp.mean(wide * wide, axis=-1, keepdims=True) + 1e-06)
    return (wide * factor * gain).astype(jnp.bfloat16)


def combine_parts(first, second):
    peak_a, total_a, accum_a = first
    peak_b, total_b, accum_b = second
    peak = jnp.maximum(peak_a, peak_b)
    factor_a = jnp.exp(peak_a - peak)
    factor_b = jnp.exp(peak_b - peak)
    return (
        peak,
        total_a * factor_a + total_b * factor_b,
        accum_a * factor_a[..., None] + accum_b * factor_b[..., None],
    )


def partial_softmax(queries, keys, values, usable, inv_root):
    scores = (
        jnp.einsum("rhe,rnhe->rhn", queries, keys, preferred_element_type=jnp.float32) * inv_root
    )
    scores = jnp.where(usable[:, None, :], scores, neg_fill)
    peak = jnp.max(scores, axis=-1)
    expo = jnp.where(usable[:, None, :], jnp.exp(scores - peak[..., None]), 0.0)
    total = jnp.sum(expo, axis=-1)
    accum = jnp.einsum("rhn,rnhe->rhe", expo, values, preferred_element_type=jnp.float32)
    return (peak, total, accum)


def split_heads(block):
    return block.reshape(block.shape[:-1] + (H, block.shape[-1] // H))


def body(
    kv_cache,
    keep_flags,
    block_weights,
    lengths,
    token_qkv,
    stream,
    w_out,
    w_up,
    w_down,
    w_qkv,
    mlp_gain,
    next_gain,
):
    seq_count = lax.axis_size("seq")
    seq_here = lax.axis_index("seq")
    reqs = kv_cache.shape[1]
    rows = kv_cache.shape[2]
    width = kv_cache.shape[3]
    head_size = width // H
    inv_root = 1.0 / math.sqrt(head_size)
    position = seq_here * rows + jnp.arange(rows, dtype=jnp.int32)
    in_range = position[None, :] < lengths[:, None]
    kept_rows = in_range & (keep_flags == 1)
    drop_rows = in_range & (keep_flags == 0)
    inclusive = jnp.cumsum(kept_rows.astype(jnp.int32), axis=1)
    held = inclusive[:, -1]
    every = lax.all_gather(held[None, :], "seq", axis=0, tiled=True)
    lower = jnp.arange(seq_count, dtype=jnp.int32)[:, None] < seq_here
    before = jnp.sum(jnp.where(lower, every, 0), axis=0)
    blocks = rows // BLK
    drop_weight = jnp.where(drop_rows, block_weights, 0.0).reshape(reqs, blocks, BLK)
    weight_total = jnp.sum(drop_weight, axis=-1)
    drop_count = jnp.sum(drop_rows.reshape(reqs, blocks, BLK).astype(jnp.int32), axis=-1)
    sums = jnp.einsum(
        "rbk,crbkd->crbd",
        drop_weight,
        kv_cache.reshape(2, reqs, blocks, BLK, width),
        preferred_element_type=jnp.float32,
        precision=lax.Precision.HIGHEST,
    )
    block_summary = (sums / jnp.maximum(weight_total, 1.0)[None, :, :, None]).astype(jnp.bfloat16)
    queries = split_heads(token_qkv[:, :width])
    own_keys = split_heads(token_qkv[:, width : 2 * width])
    own_values = split_heads(token_qkv[:, 2 * width :])
    slot = rows // seq_count
    target = jnp.arange(seq_count, dtype=jnp.int32)
    offset = jnp.mod(target[:, None] - before[None, :], seq_count)
    sent = (held[None, :] - offset + seq_count - 1) // seq_count
    wanted = offset[:, :, None] + seq_count * jnp.arange(slot, dtype=jnp.int32)[None, None, :]
    local_rank = inclusive - 1
    wanted_r = jnp.transpose(wanted, (1, 0, 2))
    pick_send = (
        kept_rows[:, None, None, :] & (local_rank[:, None, None, :] == wanted_r[:, :, :, None])
    ).astype(jnp.bfloat16)
    outgoing = jnp.einsum(
        "rtsp,crpd->ctrsd", pick_send, kv_cache, preferred_element_type=jnp.float32
    ).astype(jnp.bfloat16)
    incoming, arrived = (
        lax.all_to_all(outgoing, "seq", split_axis=1, concat_axis=1, tiled=True),
        lax.all_to_all(sent[None], "seq", split_axis=1, concat_axis=1, tiled=True),
    )
    counts_in = arrived[0]
    ends = jnp.cumsum(counts_in, axis=0)
    starts = ends - counts_in
    filled = ends[-1]
    local_rows = jnp.arange(rows, dtype=jnp.int32)
    slot_index = jnp.arange(slot, dtype=jnp.int32)
    starts_r = starts.T
    counts_r = counts_in.T
    valid_slot = slot_index[None, None, :] < counts_r[:, :, None]
    dest_row = starts_r[:, :, None] + slot_index[None, None, :]
    pick_recv = (
        valid_slot[:, None, :, :] & (dest_row[:, None, :, :] == local_rows[None, :, None, None])
    ).astype(jnp.bfloat16)
    packed_cache = jnp.einsum(
        "rlts,ctrsd->crld", pick_recv, incoming, preferred_element_type=jnp.float32
    ).astype(jnp.bfloat16)
    present = local_rows[None, :] < filled[:, None]
    row_part = partial_softmax(
        queries, split_heads(packed_cache[0]), split_heads(packed_cache[1]), present, inv_root
    )
    summary_part = partial_softmax(
        queries,
        split_heads(block_summary[0]),
        split_heads(block_summary[1]),
        drop_count > 0,
        inv_root,
    )
    peak, total, accum = combined_all(combine_parts(row_part, summary_part), "seq", combine_parts)
    own_score = (
        jnp.einsum("rhe,rhe->rh", queries, own_keys, preferred_element_type=jnp.float32) * inv_root
    )
    top_score = jnp.maximum(peak, own_score)
    factor_old = jnp.exp(peak - top_score)
    factor_own = jnp.exp(own_score - top_score)
    attended = (
        accum * factor_old[..., None] + factor_own[..., None] * own_values.astype(jnp.float32)
    ) / (total * factor_old + factor_own)[..., None]
    attended = attended.reshape(reqs, width).astype(jnp.bfloat16)
    fsdp_here = lax.axis_index("fsdp")

    def widen(columns):
        return lax.all_gather(columns, "fsdp", axis=1, tiled=True)

    def own_columns(full, count):
        return lax.dynamic_slice_in_dim(full, fsdp_here * count, count, 1)

    attn_all, stream_all = (
        lax.all_gather(attended, "fsdp", axis=0, tiled=True),
        lax.all_gather(stream, "fsdp", axis=0, tiled=True),
    )
    mid_cols = own_columns(stream_all, w_out.shape[1]).astype(jnp.float32) + jnp.dot(
        attn_all, w_out, preferred_element_type=jnp.float32
    )
    mid = widen(mid_cols.astype(jnp.bfloat16))
    hidden = widen(
        jax.nn.silu(
            jnp.dot(normalize(mid, mlp_gain), w_up, preferred_element_type=jnp.float32)
        ).astype(jnp.bfloat16)
    )
    out_cols = own_columns(mid, w_down.shape[1]).astype(jnp.float32) + jnp.dot(
        hidden, w_down, preferred_element_type=jnp.float32
    )
    layer_all = widen(out_cols.astype(jnp.bfloat16))
    qkv_all = widen(
        jnp.dot(normalize(layer_all, next_gain), w_qkv, preferred_element_type=jnp.float32).astype(
            jnp.bfloat16
        )
    )
    layer_rows = lax.dynamic_slice_in_dim(layer_all, fsdp_here * reqs, reqs, 0)
    qkv_rows = lax.dynamic_slice_in_dim(qkv_all, fsdp_here * reqs, reqs, 0)
    layer_width = width // seq_count
    qkv_width = 3 * width // seq_count
    layer_out = lax.dynamic_slice_in_dim(layer_rows, seq_here * layer_width, layer_width, 1)
    next_qkv = lax.dynamic_slice_in_dim(qkv_rows, seq_here * qkv_width, qkv_width, 1)
    return (packed_cache, block_summary, layer_out, next_qkv)


def solution(mesh):
    placed = (
        P(None, "fsdp", "seq", None),
        P("fsdp", "seq"),
        P("fsdp", "seq"),
        P("fsdp"),
        P("fsdp", None),
        P("fsdp", None),
        P(None, "fsdp"),
        P(None, "fsdp"),
        P(None, "fsdp"),
        P(None, "fsdp"),
        P(),
        P(),
    )
    return jax.shard_map(
        body,
        mesh=mesh,
        in_specs=placed,
        out_specs=(
            P(None, "fsdp", "seq", None),
            P(None, "fsdp", "seq", None),
            P("fsdp", "seq"),
            P("fsdp", "seq"),
        ),
        check_vma=False,
    )
```

profile of v0, /device:TPU:1, one launch (start us, length us, event | category | flops | bytes accessed | tf_op | source)
XLA Modules:
  0.0 290.0 jit_solution(1825323752103344393)
XLA Ops:
  2.8 1.3 dynamic-slice
  4.8 13.9 %all-reduce = s32[32]{0:T(128)S(1)} all-reduce(s32[32]{0:T(128)S(1)} %bitcast_dynamic-update-slice_fusion), channel_id=2, replica_groups=mesh['seq'=16,'fsdp'=16] {'seq'}, use_global_device_ids=true, to_apply=%add | all-reduce | flops 32 | bytes 256
  19.6 3.5 %all-to-all-start.1 = ((s32[1,16,2]{2,0,1:T(1,128)}), s32[1,16,2]{2,0,1:T(1,128)S(1)}, u32[]{:S(2)}, u32[]{:S(2)}) async-start(s32[1,16,2]{2,0,1:T(1,128)} %and_select_fusion), calls=%async_computation.1 | async-start | bytes 16384 | tf_op jit(solution)/shard_map/all_to_all | solution.py:118
  23.2 5.4 %fusion.7 = bf16[2,16,2,32,1280]{4,3,1,0,2:T(8,128)(2,1)S(1)} fusion(s32[2,16,32]{2,1,0:T(8,128)S(1)} %broadcast_add_fusion, s32[2,512]{1,0:T(2,128)S(1)} %broadcast_add_fusion.1, pred[2,512]{1,0:T(4,128)(4,1)S(1)} %get-tuple-element.236, bf16[2,2,512,1280]{3,2,1,0:T(8,128)(2,1)} %param.14), kind=kOutput, calls=%fused_computation.15 | convolution fusion | flops 2688024576 | bytes 10494976 | tf_op jit(solution)/shard_map/rtsp,crpd->ctrsd/dot_general | solution.py:113
  28.6 2.8 copy.45
  31.5 6.8 %all-to-all-start = ((bf16[2,16,2,32,1280]{4,3,0,2,1:T(8,128)(2,1)}), bf16[2,16,2,32,1280]{4,3,0,2,1:T(8,128)(2,1)}, u32[]{:S(2)}, u32[]{:S(2)}) async-start(bf16[2,16,2,32,1280]{4,3,0,2,1:T(8,128)(2,1)} %copy.45), calls=%async_computation | async-start | bytes 10485760 | tf_op jit(solution)/shard_map/all_to_all | solution.py:117
  38.8 4.8 %fusion.5 = f32[2,32,1,2,1280]{4,2,3,1,0:T(1,128)S(1)} fusion(f32[2,32,16,1,1]{2,3,4,1,0:T(1,128)S(1)} %bitcast.193, bf16[2,2,32,16,1280]{4,3,2,1,0:T(8,128)(2,1)} %bitcast.190), kind=kOutput, calls=%fused_computation.13 | convolution fusion | flops 31457280 | bytes 5902336 | tf_op jit(solution)/shard_map/rbk,crbkd->crbd/dot_general | solution.py:92
  45.6 24.9 %all-gather.2 = bf16[16,2,1280]{2,1,0:T(2,128)(2,1)S(1)} all-gather(bf16[1,2,1280]{2,1,0:T(2,128)(2,1)S(1)} %bitcast.202), channel_id=1, replica_groups=mesh['seq'=16,'fsdp'=16] {'fsdp'}, dimensions={0}, use_global_device_ids=true | all-gather | bytes 87040 | tf_op jit(solution)/shard_map/all_gather | solution.py:168
  73.7 30.8 %all-to-all-done = bf16[2,16,2,32,1280]{4,3,0,2,1:T(8,128)(2,1)} async-done(((bf16[2,16,2,32,1280]{4,3,0,2,1:T(8,128)(2,1)}), bf16[2,16,2,32,1280]{4,3,0,2,1:T(8,128)(2,1)}, u32[]{:S(2)}, u32[]{:S(2)}) %all-to-all-start) | async-done | bytes 5242912 | tf_op jit(solution)/shard_map/all_to_all | solution.py:117
  104.5 5.7 %fusion.12 = bf16[2,2,1280,512,1]{3,2,1,0,4:T(8,128)(2,1)S(1)} fusion(bf16[2,16,2,32,1280]{4,3,0,2,1:T(8,128)(2,1)} %all-to-all-done, s32[2,16,32]{2,0,1:T(2,128)S(1)} %iota_add_fusion, pred[2,16,32]{2,0,1:T(4,128)(4,1)S(1)} %iota_compare_fusion.1), kind=kOutput, calls=%fused_computation.19 | convolution fusion | flops 2685403136 | bytes 10490880 | tf_op jit(solution)/shard_map/rlts,ctrsd->crld/dot_general | solution.py:133
  110.9 1.9 copy-done.1
  115.4 7.9 %copy.55 = bf16[2,2,512,1280]{3,2,1,0:T(8,128)(2,1)} copy(bf16[2,2,512,1280]{2,3,1,0:T(8,128)(2,1)} %bitcast.188) | data formatting | bytes 10485760
  123.3 1.5 fusion.49
  125.7 18.9 %all-gather.1 = f32[32,16,80]{2,1,0:T(8,128)S(1)} all-gather(f32[2,16,80]{2,1,0:T(8,128)S(1)} %multiply_add_fusion), channel_id=3, replica_groups=mesh['seq'=16,'fsdp'=16] {'seq'}, dimensions={0}, use_global_device_ids=true | all-gather | bytes 174080 | tf_op jit(solution)/shard_map/all_gather | solution.py:13
  145.3 16.3 %all_gather.38 = f32[16,2,16]{2,1,0:T(2,128)S(1)} all-gather(f32[1,2,16]{2,1,0:T(2,128)S(1)} %get-tuple-element.239), channel_id=1, replica_groups=mesh['seq'=16,'fsdp'=16] {'seq'}, dimensions={0}, use_global_device_ids=true | all-gather | bytes 2176 | tf_op jit(solution)/shard_map/all_gather | solution.py:13
  161.6 16.5 %all_gather.37 = f32[16,2,16]{2,1,0:T(2,128)S(1)} all-gather(f32[1,2,16]{2,1,0:T(2,128)S(1)} %get-tuple-element.240), channel_id=1, replica_groups=mesh['seq'=16,'fsdp'=16] {'seq'}, dimensions={0}, use_global_device_ids=true | all-gather | bytes 2176 | tf_op jit(solution)/shard_map/all_gather | solution.py:13
  178.1 1.5 while.19
  180.5 41.5 %all-gather.3 = bf16[16,2,1280]{2,1,0:T(2,128)(2,1)S(1)} all-gather(bf16[1,2,1280]{2,1,0:T(2,128)(2,1)S(1)} %reshape.375), channel_id=1, replica_groups=mesh['seq'=16,'fsdp'=16] {'fsdp'}, dimensions={0}, use_global_device_ids=true | all-gather | bytes 87040 | tf_op jit(solution)/shard_map/all_gather | solution.py:167
  222.3 14.8 %all-gather.4 = bf16[16,80,32]{1,2,0:T(8,128)(2,1)S(1)} all-gather(bf16[1,80,32]{1,2,0:T(8,128)(2,1)S(1)} %fusion.21), channel_id=1, replica_groups=mesh['seq'=16,'fsdp'=16] {'fsdp'}, dimensions={0}, use_global_device_ids=true | all-gather | bytes 87040 | tf_op jit(solution)/shard_map/all_gather | solution.py:161
  237.4 1.2 fusion.57
  238.7 16.1 %all-gather.5 = bf16[16,80,32]{1,2,0:T(8,128)(2,1)S(1)} all-gather(bf16[1,80,32]{1,2,0:T(8,128)(2,1)S(1)} %fusion.57), channel_id=1, replica_groups=mesh['seq'=16,'fsdp'=16] {'fsdp'}, dimensions={0}, use_global_device_ids=true | all-gather | bytes 87040 | tf_op jit(solution)/shard_map/all_gather | solution.py:161
  255.0 1.1 fusion.20
  256.2 14.8 %all-gather.6 = bf16[16,80,32]{1,2,0:T(8,128)(2,1)S(1)} all-gather(bf16[1,80,32]{1,2,0:T(8,128)(2,1)S(1)} %fusion.20), channel_id=1, replica_groups=mesh['seq'=16,'fsdp'=16] {'fsdp'}, dimensions={0}, use_global_device_ids=true | all-gather | bytes 87040 | tf_op jit(solution)/shard_map/all_gather | solution.py:161
  271.6 16.6 %all-gather.7 = bf16[16,240,32]{1,2,0:T(8,128)(2,1)S(1)} all-gather(bf16[1,240,32]{1,2,0:T(8,128)(2,1)S(1)} %fusion.17), channel_id=1, replica_groups=mesh['seq'=16,'fsdp'=16] {'fsdp'}, dimensions={0}, use_global_device_ids=true | all-gather | bytes 261120 | tf_op jit(solution)/shard_map/all_gather | solution.py:161
  (136 shorter events, 19.2 us)
Async XLA Ops:
  0.6 270.7 %copy-start = (bf16[1280,240]{0,1:T(8,128)(2,1)S(1)}, bf16[1280,240]{0,1:T(8,128)(2,1)}, u32[]{:S(2)}) copy-start(bf16[1280,240]{0,1:T(8,128)(2,1)} %param.23) | copy-start | bytes 1843204
  19.6 11.9 %all-to-all-start.1 = ((s32[1,16,2]{2,0,1:T(1,128)}), s32[1,16,2]{2,0,1:T(1,128)S(1)}, u32[]{:S(2)}, u32[]{:S(2)}) async-start(s32[1,16,2]{2,0,1:T(1,128)} %and_select_fusion), calls=%async_computation.1 | async-start | bytes 16384 | tf_op jit(solution)/shard_map/all_to_all | solution.py:118
  31.5 6.8 %copy-start.10 = (f32[2,512]{1,0:T(2,128)S(1)}, f32[2,512]{1,0:T(2,128)}, u32[]{:S(2)}) copy-start(f32[2,512]{1,0:T(2,128)} %param.16) | copy-start | bytes 12292
  31.5 7.0 %copy-start.7 = (bf16[2,3840]{1,0:T(2,128)(2,1)S(1)}, bf16[2,3840]{1,0:T(2,128)(2,1)}, u32[]{:S(2)}) copy-start(bf16[2,3840]{1,0:T(2,128)(2,1)} %param.18) | copy-start | bytes 46084
  31.5 73.0 %all-to-all-start = ((bf16[2,16,2,32,1280]{4,3,0,2,1:T(8,128)(2,1)}), bf16[2,16,2,32,1280]{4,3,0,2,1:T(8,128)(2,1)}, u32[]{:S(2)}, u32[]{:S(2)}) async-start(bf16[2,16,2,32,1280]{4,3,0,2,1:T(8,128)(2,1)} %copy.45), calls=%async_computation | async-start | bytes 10485760 | tf_op jit(solution)/shard_map/all_to_all | solution.py:117
  38.3 7.3 %copy-start.9 = (bf16[2,1280]{1,0:T(2,128)(2,1)S(1)}, bf16[2,1280]{1,0:T(2,128)(2,1)}, u32[]{:S(2)}) copy-start(bf16[2,1280]{1,0:T(2,128)(2,1)} %param.19) | copy-start | bytes 15364
  43.7 0.7 copy-start.2
  71.6 38.6 %copy-start.4 = (f32[2,16]{1,0:T(2,128)}, f32[2,16]{1,0:T(2,128)S(1)}, u32[]{:S(2)}) copy-start(f32[2,16]{1,0:T(2,128)S(1)} %fusion.60) | copy-start | bytes 388
  110.5 2.3 copy-start.1
  110.5 3.5 %copy-start.5 = (f32[2,16]{1,0:T(2,128)S(1)}, f32[2,16]{1,0:T(2,128)}, u32[]{:S(2)}) copy-start(f32[2,16]{1,0:T(2,128)} %copy-done.4) | copy-start | bytes 388
  115.4 29.2 %copy-start.6 = (f32[2,16]{1,0:T(2,128)S(1)}, f32[2,16]{1,0:T(2,128)}, u32[]{:S(2)}) copy-start(f32[2,16]{1,0:T(2,128)} %copy-done.4) | copy-start | bytes 388
  115.4 106.6 %copy-start.3 = (bf16[1280,80]{0,1:T(8,128)(2,1)S(1)}, bf16[1280,80]{0,1:T(8,128)(2,1)}, u32[]{:S(2)}) copy-start(bf16[1280,80]{0,1:T(8,128)(2,1)} %param.20) | copy-start | bytes 614404
  123.3 148.0 %copy-start.8 = (f32[1280]{0:T(1024)S(1)}, f32[1280]{0:T(1024)}, u32[]{:S(2)}) copy-start(f32[1280]{0:T(1024)} %param.25) | copy-start | bytes 15364
where the time goes:
time: 291 us; the launch traced here: 290 us
  blocking collectives  194 us (67%)
  waiting for transfers between devices  30.8 us (11%)
  matrix products  21.6 us (7%)
  local copies, waits for them, and re-layouts  20.2 us (7%)
  other arithmetic  11 us (4%)
  starting transfers between devices  10.2 us (4%)
    all_gather x4, blocking collectives, widen(): return lax.all_gather(columns, 'fsdp', axis=1, tiled=True)  62.3 us
    all_gather x3, blocking collectives, combined_all(): gathered = jax.tree.map(lambda a: lax.all_gather(a, axis), part)  51.7 us
    all_gather x1, blocking collectives, body(): lax.all_gather(attended, 'fsdp', axis=0, tiled=True)  41.5 us
    all_to_all x1, waiting for transfers between devices, body(): lax.all_to_all(outgoing, 'seq', split_axis=1, concat_axis=1, tiled=True)  30.8 us
    all_gather x1, blocking collectives, body(): lax.all_gather(stream, 'fsdp', axis=0, tiled=True)  24.9 us
    unnamed x1, blocking collectives  13.9 us
    unnamed x35, local copies, waits for them, and re-layouts  13.1 us
    all_to_all x1, starting transfers between devices, body(): lax.all_to_all(outgoing, 'seq', split_axis=1, concat_axis=1, tiled=True)  6.77 us
  transfers between devices with their start and end apart: 2, of which 1 were waited for; matrix products, arithmetic and copies ran while one was open for 6% of the time, Pallas kernels for 0%

commit v1 on v0

--- a/solution.py
+++ b/solution.py
@@ -158,7 +158,9 @@
     fsdp_here = lax.axis_index("fsdp")
 
     def widen(columns):
-        return lax.all_gather(columns, "fsdp", axis=1, tiled=True)
+        return jnp.concatenate(
+            lax.all_to_all(jnp.stack([columns] * lax.axis_size("fsdp")), "fsdp", 0, 0), axis=1
+        )
 
     def own_columns(full, count):
         return lax.dynamic_slice_in_dim(full, fsdp_here * count, count, 1)

time: 291 us -> 265 us (0.911)
  blocking collectives: 194 us -> 168 us
  waiting for transfers between devices: 30.8 us -> 36 us
  other arithmetic: 11 us -> 5.97 us
  starting transfers between devices: 10.2 us -> 13.7 us
  matrix products: 21.6 us -> 18.4 us
    all_gather x4 -> x0, blocking collectives: 62.3 us -> none  [widen(): return lax.all_gather(columns, 'fsdp', axis=1, tiled=True)]
    all_to_all x0 -> x3, blocking collectives: none -> 36 us  [widen(): lax.all_to_all(jnp.stack([columns] * lax.axis_size('fsdp')), 'fsdp', 0, 0)]
    all_to_all x0 -> x1, starting transfers between devices: none -> 3.43 us  [widen(): lax.all_to_all(jnp.stack([columns] * lax.axis_size('fsdp')), 'fsdp', 0, 0)]
    unnamed x35 -> x31, local copies, waits for them, and re-layouts: 13.1 us -> 11.5 us
  transfers between devices with their start and end apart: 2 -> 3, of which waited for: 1 -> 2; matrix products, arithmetic and copies ran while one was open for 6% -> 9% of each run, Pallas kernels for 0% -> 0%
where the time goes in v1:
time: 265 us; the launch traced here: 264 us
  blocking collectives  168 us (63%)
  waiting for transfers between devices  36 us (14%)
  local copies, waits for them, and re-layouts  20.4 us (8%)
  matrix products  18.4 us (7%)
  starting transfers between devices  13.7 us (5%)
  other arithmetic  5.97 us (2%)
    all_gather x3, blocking collectives, combined_all(): gathered = jax.tree.map(lambda a: lax.all_gather(a, axis), part)  51.9 us
    all_gather x1, blocking collectives, body(): lax.all_gather(attended, 'fsdp', axis=0, tiled=True)  41.4 us
    all_to_all x3, blocking collectives, widen(): lax.all_to_all(jnp.stack([columns] * lax.axis_size('fsdp')), 'fsdp', 0, 0)  36 us
    all_to_all x1, waiting for transfers between devices, body(): lax.all_to_all(outgoing, 'seq', split_axis=1, concat_axis=1, tiled=True)  33.3 us
    all_gather x1, blocking collectives, body(): lax.all_gather(stream, 'fsdp', axis=0, tiled=True)  24.9 us
    unnamed x1, blocking collectives  13.9 us
    unnamed x31, local copies, waits for them, and re-layouts  11.5 us
    all_to_all x1, starting transfers between devices, body(): lax.all_to_all(outgoing, 'seq', split_axis=1, concat_axis=1, tiled=True)  6.77 us
  transfers between devices with their start and end apart: 3, of which 2 were waited for; matrix products, arithmetic and copies ran while one was open for 9% of the time, Pallas kernels for 0%

profile of v1, /device:TPU:1, one launch (start us, length us, event | category | flops | bytes accessed | tf_op | source)
XLA Modules:
  0.0 264.2 jit_solution(14141005807466823765)
XLA Ops:
  0.7 0.8 fusion.59
  2.8 1.3 dynamic-slice
  4.8 13.9 %all-reduce = s32[32]{0:T(128)S(1)} all-reduce(s32[32]{0:T(128)S(1)} %bitcast_dynamic-update-slice_fusion), channel_id=2, replica_groups=mesh['seq'=16,'fsdp'=16] {'seq'}, use_global_device_ids=true, to_apply=%add | all-reduce | flops 32 | bytes 256
  19.6 3.5 %all-to-all-start.1 = ((s32[1,16,2]{2,0,1:T(1,128)}), s32[1,16,2]{2,0,1:T(1,128)S(1)}, u32[]{:S(2)}, u32[]{:S(2)}) async-start(s32[1,16,2]{2,0,1:T(1,128)} %and_select_fusion), calls=%async_computation.1 | async-start | bytes 16384 | tf_op jit(solution)/shard_map/all_to_all | solution.py:118
  23.2 5.4 %fusion.9 = bf16[2,16,2,32,1280]{4,3,1,0,2:T(8,128)(2,1)S(1)} fusion(s32[2,16,32]{2,1,0:T(8,128)S(1)} %broadcast_add_fusion, s32[2,512]{1,0:T(2,128)S(1)} %broadcast_add_fusion.1, pred[2,512]{1,0:T(4,128)(4,1)S(1)} %get-tuple-element.240, bf16[2,2,512,1280]{3,2,1,0:T(8,128)(2,1)} %param.14), kind=kOutput, calls=%fused_computation.17 | convolution fusion | flops 2688024576 | bytes 10494976 | tf_op jit(solution)/shard_map/rtsp,crpd->ctrsd/dot_general | solution.py:113
  28.6 2.8 %copy.52 = bf16[2,16,2,32,1280]{4,3,0,2,1:T(8,128)(2,1)} copy(bf16[2,16,2,32,1280]{4,3,1,0,2:T(8,128)(2,1)S(1)} %fusion.9) | data formatting | bytes 10485760 | tf_op jit(solution)/shard_map/convert_element_type | solution.py:115
  31.5 6.8 %all-to-all-start = ((bf16[2,16,2,32,1280]{4,3,0,2,1:T(8,128)(2,1)}), bf16[2,16,2,32,1280]{4,3,0,2,1:T(8,128)(2,1)}, u32[]{:S(2)}, u32[]{:S(2)}) async-start(bf16[2,16,2,32,1280]{4,3,0,2,1:T(8,128)(2,1)} %copy.52), calls=%async_computation | async-start | bytes 10485760 | tf_op jit(solution)/shard_map/all_to_all | solution.py:117
  38.8 4.8 %fusion.5 = f32[2,32,1,2,1280]{4,2,3,1,0:T(1,128)S(1)} fusion(f32[2,32,16,1,1]{2,3,4,1,0:T(1,128)S(1)} %bitcast.158, bf16[2,2,32,16,1280]{4,3,2,1,0:T(8,128)(2,1)} %bitcast.151), kind=kOutput, calls=%fused_computation.13 | convolution fusion | flops 31457280 | bytes 5902336 | tf_op jit(solution)/shard_map/rbk,crbkd->crbd/dot_general | solution.py:92
  44.9 24.9 %all-gather.2 = bf16[16,2,1280]{2,1,0:T(2,128)(2,1)S(1)} all-gather(bf16[1,2,1280]{2,1,0:T(2,128)(2,1)S(1)} %bitcast.167), channel_id=1, replica_groups=mesh['seq'=16,'fsdp'=16] {'fsdp'}, dimensions={0}, use_global_device_ids=true | all-gather | bytes 87040 | tf_op jit(solution)/shard_map/all_gather | solution.py:170
  71.2 33.3 %all-to-all-done = bf16[2,16,2,32,1280]{4,3,0,2,1:T(8,128)(2,1)} async-done(((bf16[2,16,2,32,1280]{4,3,0,2,1:T(8,128)(2,1)}), bf16[2,16,2,32,1280]{4,3,0,2,1:T(8,128)(2,1)}, u32[]{:S(2)}, u32[]{:S(2)}) %all-to-all-start) | async-done | bytes 5242912 | tf_op jit(solution)/shard_map/all_to_all | solution.py:117
  104.5 5.7 %fusion.7 = bf16[2,2,1280,512,1]{3,2,0,1,4:T(8,128)(2,1)S(1)} fusion(bf16[2,16,2,32,1280]{4,3,0,2,1:T(8,128)(2,1)} %all-to-all-done, s32[2,16,32]{2,0,1:T(2,128)S(1)} %iota_add_fusion, pred[2,16,32]{2,0,1:T(4,128)(4,1)S(1)} %iota_compare_fusion.1), kind=kOutput, calls=%fused_computation.15 | convolution fusion | flops 2685403136 | bytes 10490880 | tf_op jit(solution)/shard_map/rlts,ctrsd->crld/dot_general | solution.py:133
  110.9 1.9 copy-done.1
  114.5 18.9 %all-gather.1 = f32[32,16,80]{2,1,0:T(8,128)S(1)} all-gather(f32[2,16,80]{2,1,0:T(8,128)S(1)} %multiply_add_fusion), channel_id=3, replica_groups=mesh['seq'=16,'fsdp'=16] {'seq'}, dimensions={0}, use_global_device_ids=true | all-gather | bytes 174080 | tf_op jit(solution)/shard_map/all_gather | solution.py:13
  133.5 16.3 %all_gather.26 = f32[16,2,16]{2,1,0:T(2,128)S(1)} all-gather(f32[1,2,16]{2,1,0:T(2,128)S(1)} %get-tuple-element.243), channel_id=1, replica_groups=mesh['seq'=16,'fsdp'=16] {'seq'}, dimensions={0}, use_global_device_ids=true | all-gather | bytes 2176 | tf_op jit(solution)/shard_map/all_gather | solution.py:13
  149.8 16.7 %all_gather.25 = f32[16,2,16]{2,1,0:T(2,128)S(1)} all-gather(f32[1,2,16]{2,1,0:T(2,128)S(1)} %get-tuple-element.244), channel_id=1, replica_groups=mesh['seq'=16,'fsdp'=16] {'seq'}, dimensions={0}, use_global_device_ids=true | all-gather | bytes 2176 | tf_op jit(solution)/shard_map/all_gather | solution.py:13
  166.5 1.5 while.19
  168.2 41.4 %all-gather.3 = bf16[16,2,1280]{2,1,0:T(2,128)(2,1)S(1)} all-gather(bf16[1,2,1280]{2,1,0:T(2,128)(2,1)S(1)} %reshape.415), channel_id=1, replica_groups=mesh['seq'=16,'fsdp'=16] {'fsdp'}, dimensions={0}, use_global_device_ids=true | all-gather | bytes 87040 | tf_op jit(solution)/shard_map/all_gather | solution.py:169
  209.8 12.8 %all_to_all.30 = bf16[16,32,80]{2,1,0:T(8,128)(2,1)S(1)} all-to-all(bf16[16,32,80]{2,1,0:T(8,128)(2,1)S(1)} %stack.8), channel_id=1, replica_groups=mesh['seq'=16,'fsdp'=16] {'fsdp'}, dimensions={0} | all-to-all | bytes 163840 | tf_op jit(solution)/shard_map/all_to_all | solution.py:162
  223.3 11.6 %all_to_all.31 = bf16[16,32,80]{2,1,0:T(8,128)(2,1)S(1)} all-to-all(bf16[16,32,80]{2,1,0:T(8,128)(2,1)S(1)} %stack.9), channel_id=1, replica_groups=mesh['seq'=16,'fsdp'=16] {'fsdp'}, dimensions={0} | all-to-all | bytes 163840 | tf_op jit(solution)/shard_map/all_to_all | solution.py:162
  235.3 11.6 %all_to_all.32 = bf16[16,32,80]{2,1,0:T(8,128)(2,1)S(1)} all-to-all(bf16[16,32,80]{2,1,0:T(8,128)(2,1)S(1)} %stack.10), channel_id=1, replica_groups=mesh['seq'=16,'fsdp'=16] {'fsdp'}, dimensions={0} | all-to-all | bytes 163840 | tf_op jit(solution)/shard_map/all_to_all | solution.py:162
  247.6 0.8 stack.11
  248.4 3.4 %all-to-all-start.5 = ((bf16[16,32,240]{2,1,0:T(8,128)(2,1)}), bf16[16,32,240]{2,1,0:T(8,128)(2,1)S(1)}, u32[]{:S(2)}, u32[]{:S(2)}) async-start(bf16[16,32,240]{2,1,0:T(8,128)(2,1)} %stack.11), calls=%async_computation.5 | async-start | bytes 524288 | tf_op jit(solution)/shard_map/all_to_all | solution.py:162
  251.9 7.9 %copy.61 = bf16[2,2,512,1280]{3,2,1,0:T(8,128)(2,1)} copy(bf16[2,2,512,1280]{2,3,0,1:T(8,128)(2,1)} %bitcast.149) | data formatting | bytes 10485760
  260.3 2.7 %all-to-all-done.5 = bf16[16,32,240]{2,1,0:T(8,128)(2,1)S(1)} async-done(((bf16[16,32,240]{2,1,0:T(8,128)(2,1)}), bf16[16,32,240]{2,1,0:T(8,128)(2,1)S(1)}, u32[]{:S(2)}, u32[]{:S(2)}) %all-to-all-start.5) | async-done | bytes 245792 | tf_op jit(solution)/shard_map/all_to_all | solution.py:162
  (141 shorter events, 13.3 us)
Async XLA Ops:
  0.6 246.7 %copy-start = (bf16[1280,240]{0,1:T(8,128)(2,1)S(1)}, bf16[1280,240]{0,1:T(8,128)(2,1)}, u32[]{:S(2)}) copy-start(bf16[1280,240]{0,1:T(8,128)(2,1)} %param.23) | copy-start | bytes 1843204
  19.6 11.9 %all-to-all-start.1 = ((s32[1,16,2]{2,0,1:T(1,128)}), s32[1,16,2]{2,0,1:T(1,128)S(1)}, u32[]{:S(2)}, u32[]{:S(2)}) async-start(s32[1,16,2]{2,0,1:T(1,128)} %and_select_fusion), calls=%async_computation.1 | async-start | bytes 16384 | tf_op jit(solution)/shard_map/all_to_all | solution.py:118
  31.5 6.8 %copy-start.8 = (f32[2,512]{1,0:T(2,128)S(1)}, f32[2,512]{1,0:T(2,128)}, u32[]{:S(2)}) copy-start(f32[2,512]{1,0:T(2,128)} %param.16) | copy-start | bytes 12292
  31.5 7.0 %copy-start.5 = (bf16[2,3840]{1,0:T(2,128)(2,1)S(1)}, bf16[2,3840]{1,0:T(2,128)(2,1)}, u32[]{:S(2)}) copy-start(bf16[2,3840]{1,0:T(2,128)(2,1)} %param.18) | copy-start | bytes 46084
  31.5 73.0 %all-to-all-start = ((bf16[2,16,2,32,1280]{4,3,0,2,1:T(8,128)(2,1)}), bf16[2,16,2,32,1280]{4,3,0,2,1:T(8,128)(2,1)}, u32[]{:S(2)}, u32[]{:S(2)}) async-start(bf16[2,16,2,32,1280]{4,3,0,2,1:T(8,128)(2,1)} %copy.52), calls=%async_computation | async-start | bytes 10485760 | tf_op jit(solution)/shard_map/all_to_all | solution.py:117
  38.3 6.6 %copy-start.7 = (bf16[2,1280]{1,0:T(2,128)(2,1)S(1)}, bf16[2,1280]{1,0:T(2,128)(2,1)}, u32[]{:S(2)}) copy-start(bf16[2,1280]{1,0:T(2,128)(2,1)} %param.19) | copy-start | bytes 15364
  43.7 66.5 %copy-start.2 = (bf16[2,2,32,1280]{3,2,1,0:T(8,128)(2,1)}, bf16[2,2,32,1280]{3,2,1,0:T(8,128)(2,1)S(1)}, u32[]{:S(2)}) copy-start(bf16[2,2,32,1280]{3,2,1,0:T(8,128)(2,1)S(1)} %fusion.26) | copy-start | bytes 983044
  110.5 2.3 copy-start.1
  112.8 96.7 %copy-start.3 = (bf16[1280,80]{0,1:T(8,128)(2,1)S(1)}, bf16[1280,80]{0,1:T(8,128)(2,1)}, u32[]{:S(2)}) copy-start(bf16[1280,80]{0,1:T(8,128)(2,1)} %param.20) | copy-start | bytes 614404
  112.8 110.1 %copy-start.9 = (bf16[1280,80]{0,1:T(8,128)(2,1)S(1)}, bf16[1280,80]{0,1:T(8,128)(2,1)}, u32[]{:S(2)}) copy-start(bf16[1280,80]{0,1:T(8,128)(2,1)} %param.21) | copy-start | bytes 614404
  112.8 110.1 %copy-start.10 = (f32[1280]{0:T(1024)S(1)}, f32[1280]{0:T(1024)}, u32[]{:S(2)}) copy-start(f32[1280]{0:T(1024)} %param.24) | copy-start | bytes 15364
  112.8 122.3 %copy-start.4 = (bf16[1280,80]{0,1:T(8,128)(2,1)S(1)}, bf16[1280,80]{0,1:T(8,128)(2,1)}, u32[]{:S(2)}) copy-start(bf16[1280,80]{0,1:T(8,128)(2,1)} %param.22) | copy-start | bytes 614404
  112.9 134.5 %copy-start.6 = (f32[1280]{0:T(1024)S(1)}, f32[1280]{0:T(1024)}, u32[]{:S(2)}) copy-start(f32[1280]{0:T(1024)} %param.25) | copy-start | bytes 15364
  248.4 14.6 %all-to-all-start.5 = ((bf16[16,32,240]{2,1,0:T(8,128)(2,1)}), bf16[16,32,240]{2,1,0:T(8,128)(2,1)S(1)}, u32[]{:S(2)}, u32[]{:S(2)}) async-start(bf16[16,32,240]{2,1,0:T(8,128)(2,1)} %stack.11), calls=%async_computation.5 | async-start | bytes 524288 | tf_op jit(solution)/shard_map/all_to_all | solution.py:162
